TPU v7x, 32 devices: a whole 2x2x4 slice. The times are simulated.
32 devices in a mesh: row: 8 (over z, x), col: 2 (over y), tm: 2 (over core).
Axes of the slice: x: 2, y: 2, z: 4, core: 2. Of those that a mesh axis runs over, the one named last changes fastest.
Arguments:
- queries: bfloat16 [4096, 6144], P(('row', 'tm'), 'col'), may hold values from -6 to 6
- k_cache: bfloat16 [8, 2048, 6144], P('row', 'tm', 'col'), may hold values from -6 to 6
- v_cache: bfloat16 [8, 2048, 6144], P('row', 'tm', 'col'), may hold values from -48 to 48
- lists: int32 [8, 4, 4], P('row'), may hold values from 0 to 15, all different within a row
- counts: int32 [8, 4], P('row'), may hold values from 1 to 4
- w_out: bfloat16 [6144, 6144], P('row', 'col'), may hold values from -0.078125 to 0.078125
Outputs:
- projected: bfloat16 [4096, 6144], P(('row', 'tm'), 'col')
Inputs may be any that keep to these rules, and one draw needn't show every extreme that they name: `lists`: the 4 entries of one list name different cached blocks of the stream.
All inputs are finite; a program needn't handle non-finite values.
Results may differ from a plain program's by a relative error of at most 0.0057.
Values may be sent and summed in bfloat16 or wider, within the bound.
No kernel may reach another device: no remote copies, remote signals or barrier semaphores. Data moves between devices by JAX's collectives and lax.ppermute only.
A program may use at most 128 MiB of HBM per device.

v0:
```python
import math

import jax
import jax.numpy as jnp
from jax import lax
from jax.sharding import PartitionSpec as P

HD = 128
BLK = 128
LIST = 4


def swapped(value, axis, bit):
    mask = 2**bit
    pairs = [(source, source ^ mask) for source in range(lax.axis_size(axis))]
    return lax.ppermute(value, axis, pairs)


def attend(query_rows, key_blocks, value_blocks, block_index, entry_live):
    query_count = block_index.shape[0]
    head_count = query_rows.shape[1] // HD
    shaped = query_rows.reshape(query_count, BLK, head_count, HD)
    key_taken = key_blocks[block_index]
    value_taken = value_blocks[block_index]
    scores = jnp.einsum(
        "bqhd,bjkhd->bhqjk", shaped, key_taken, preferred_element_type=jnp.float32
    ) * (1.0 / math.sqrt(HD))
    weights = jax.nn.sigmoid(scores - math.log(LIST * BLK))
    weights = jnp.where(entry_live[:, None, None, :, None], weights, 0.0).astype(jnp.bfloat16)
    mixed = jnp.einsum(
        "bhqjk,bjkhd->bqhd", weights, value_taken, preferred_element_type=jnp.float32
    )
    return mixed.reshape(query_count * BLK, query_rows.shape[1])


def local(queries, k_cache, v_cache, lists, counts, w_out):
    own_index = lax.axis_index("tm")
    width = queries.shape[1]
    head_count = width // HD
    query_blocks = queries.shape[0] // BLK
    local_blocks = k_cache.shape[1] // BLK
    entries = jnp.arange(LIST)
    own_lists = lax.dynamic_slice_in_dim(lists[0], own_index * query_blocks, query_blocks, 0)
    own_counts = lax.dynamic_slice_in_dim(counts[0], own_index * query_blocks, query_blocks, 0)
    own_keys = k_cache[0].reshape(local_blocks, BLK, head_count, HD)
    own_values = v_cache[0].reshape(local_blocks, BLK, head_count, HD)
    peer_keys, peer_values = swapped((k_cache, v_cache), "tm", 0)
    key_blocks = jnp.concatenate(
        [own_keys, peer_keys[0].reshape(local_blocks, BLK, head_count, HD)], 0
    )
    value_blocks = jnp.concatenate(
        [own_values, peer_values[0].reshape(local_blocks, BLK, head_count, HD)], 0
    )
    owner = own_lists // local_blocks
    within = own_lists % local_blocks
    block_index = jnp.where(owner == own_index, within, local_blocks + within)
    entry_live = entries[None, :] < own_counts[:, None]
    heads_out = attend(queries, key_blocks, value_blocks, block_index, entry_live).astype(
        jnp.bfloat16
    )
    full_rows = lax.all_gather(heads_out, "col", axis=1, tiled=True)
    half_width = w_out.shape[1] // 2
    own_half = lax.dynamic_slice_in_dim(w_out, own_index * half_width, half_width, 1)
    gathered = lax.all_gather(own_half, "row", axis=0, tiled=True)
    other_half = swapped(gathered, "tm", 0)
    low_half = jnp.where(own_index == 0, gathered, other_half)
    high_half = jnp.where(own_index == 0, other_half, gathered)
    result = jnp.concatenate(
        [
            jnp.dot(full_rows, low_half, preferred_element_type=jnp.float32),
            jnp.dot(full_rows, high_half, preferred_element_type=jnp.float32),
        ],
        1,
    )
    return result.astype(jnp.bfloat16)


def solution(mesh):
    placed = (
        P(("row", "tm"), "col"),
        P("row", "tm", "col"),
        P("row", "tm", "col"),
        P("row", None, None),
        P("row", None),
        P("row", "col"),
    )
    return jax.shard_map(
        local, mesh=mesh, in_specs=placed, out_specs=P(("row", "tm"), "col"), check_vma=False
    )
```

profile of v0, /device:TPU:0, one launch (start us, length us, event | category | flops | bytes accessed | tf_op | source)
XLA Modules:
  0.0 548.7 jit_solution(12835200294608654511)
XLA Ops:
  7.4 0.0 copy-start
  7.4 0.0 copy-start.3
  7.4 0.0 all-gather.5.cloned.1.call-start
  7.4 3.2 constant_dynamic-slice_fusion
  10.6 0.0 slice-start
  10.6 0.0 all-gather.5.cloned.1.call-update
  10.6 0.0 all-gather.3.cloned.1.call-start
  10.7 365.2 %all-gather.5.cloned.1.call-done = bf16[6144,1536]{1,0:T(8,128)(2,1)} async-done(((bf16[768,1536]{1,0:T(8,128)(2,1)}), bf16[6144,1536]{1,0:T(8,128)(2,1)}) %all-gather.5.cloned.1.call-update) | async-done | bytes 18874384 | tf_op jit(solution)/shard_map/all_gather | solution.py:64
  375.9 0.0 collective-permute-start.2
  375.9 0.5 collective-permute-start
  376.4 0.0 collective-permute-start.1
  376.4 0.0 copy-done.3
  376.5 0.1 reshape.147
  376.5 0.0 slice-start.1
  376.5 4.9 copy.12
  381.4 0.0 slice-done
  381.4 0.0 slice-done.1
  381.4 0.0 copy-start.2
  381.4 4.5 copy.14
  386.0 0.0 copy-done.2
  386.0 0.3 copy.16
  386.3 0.0 copy-done
  386.3 0.1 fusion.40
  386.4 0.1 iota_compare_fusion
  386.5 27.0 %collective-permute-done = bf16[1,1024,3072]{2,1,0:T(8,128)(2,1)} collective-permute-done((bf16[1,1024,3072]{2,1,0:T(8,128)(2,1)}, bf16[1,1024,3072]{2,1,0:T(8,128)(2,1)}, u32[]{:S(2)}, u32[]{:S(2)}) %collective-permute-start) | collective-permute-done | bytes 6291488 | tf_op jit(solution)/shard_map/ppermute | solution.py:16
  413.4 4.7 copy.13
  418.1 4.3 collective-permute-done.1
  422.4 7.3 %copy.15 = bf16[128,8,24,128]{3,2,1,0:T(8,128)(2,1)} copy(bf16[128,8,24,128]{3,1,2,0:T(8,128)(2,1)} %bitcast.22) | data formatting | bytes 12582912
  429.7 5.8 %pad_maximum_fusion = bf16[16,128,24,128]{3,2,1,0:T(8,128)(2,1)} fusion(bf16[8,128,24,128]{3,2,1,0:T(8,128)(2,1)S(1)} %bitcast.59, bf16[8,128,24,128]{3,2,1,0:T(8,128)(2,1)S(1)} %bitcast.58), kind=kLoop, calls=%fused_computation.8 | loop fusion | flops 6291456 | bytes 25165824 | tf_op jit(solution)/shard_map/concatenate | solution.py:51
  435.5 8.5 %gather_fusion = bf16[8,128,24,128]{3,2,1,0:T(8,128)(2,1)} fusion(bf16[16,128,24,128]{3,2,1,0:T(8,128)(2,1)} %pad_maximum_fusion, s32[1024]{0:T(1024)S(1)} %pad_clamp_fusion), kind=kCustom, calls=%fused_computation | custom fusion | bytes 12582944 | tf_op jit(solution)/shard_map/gather | solution.py:24
  444.0 10.5 %pad_maximum_fusion.1 = bf16[16,128,24,128]{3,2,1,0:T(8,128)(2,1)} fusion(bf16[8,128,24,128]{3,2,1,0:T(8,128)(2,1)} %bitcast.60, bf16[8,128,24,128]{3,2,1,0:T(8,128)(2,1)} %bitcast.57), kind=kLoop, calls=%fused_computation.9 | loop fusion | flops 6291456 | bytes 25165824 | tf_op jit(solution)/shard_map/concatenate | solution.py:48
  454.5 8.5 %gather_fusion.1 = bf16[8,128,24,128]{3,2,1,0:T(8,128)(2,1)} fusion(bf16[16,128,24,128]{3,2,1,0:T(8,128)(2,1)} %pad_maximum_fusion.1, s32[1024]{0:T(1024)S(1)} %pad_clamp_fusion), kind=kCustom, calls=%fused_computation.1 | custom fusion | bytes 12582944 | tf_op jit(solution)/shard_map/gather | solution.py:23
  463.1 9.6 %fusion.31 = bf16[2,128,24,128]{1,3,2,0:T(8,128)(2,1)S(1)} fusion(bf16[2,4,128,24,128]{4,3,2,1,0:T(8,128)(2,1)} %bitcast.66, pred[2,4]{1,0:T(4,128)(4,1)S(1)} %iota_compare_fusion, bf16[2,128,24,128,1]{3,2,1,0,4:T(8,128)(2,1)S(1)} %bitcast.70, bf16[2,4,128,24,128]{4,3,2,1,0:T(8,128)(2,1)} %bitcast.65), kind=kOutput, calls=%fused_computation.22 | convolution fusion | flops 1633419264 | bytes 15728648 | tf_op jit(solution)/shard_map/bhqjk,bjkhd->bqhd/dot_general | solution.py:30
  472.7 1.0 copy.8
  473.7 1.5 copy.42
  475.1 0.0 all-gather.3.cloned.1.call-update
  475.2 44.9 %all-gather.3.cloned.1.call-done = bf16[256,6144]{1,0:T(8,128)(2,1)} async-done(((bf16[256,3072]{1,0:T(8,128)(2,1)}), bf16[256,6144]{1,0:T(8,128)(2,1)}) %all-gather.3.cloned.1.call-update) | async-done | bytes 3145744 | tf_op jit(solution)/shard_map/all_gather | solution.py:61
  520.0 0.0 collective-permute-done.2
  520.0 9.9 %fusion.17 = bf16[256,1536]{1,0:T(8,128)(2,1)S(1)} fusion(bf16[256,6144]{1,0:T(8,128)(2,1)} %all-gather.3.cloned.1.call-done, bf16[6144,1536]{1,0:T(8,128)(2,1)} %all-gather.5.cloned.1.call-done, bf16[6144,1536]{1,0:T(8,128)(2,1)} %collective-permute-done.2, pred[]{:T(512)S(6)} %eq.21), kind=kOutput, calls=%fused_computation.17 | convolution fusion | flops 4841668608 | bytes 41680896 | tf_op jit(solution)/shard_map/dot_general | solution.py:70
  529.9 0.0 copy-start.1
  529.9 9.9 %fusion.20 = bf16[256,1536]{1,0:T(8,128)(2,1)S(1)} fusion(bf16[256,6144]{1,0:T(8,128)(2,1)} %all-gather.3.cloned.1.call-done, bf16[6144,1536]{1,0:T(8,128)(2,1)} %collective-permute-done.2, bf16[6144,1536]{1,0:T(8,128)(2,1)} %all-gather.5.cloned.1.call-done, pred[]{:T(512)S(6)} %eq.21), kind=kOutput, calls=%fused_computation.18 | convolution fusion | flops 4841668608 | bytes 41680896 | tf_op jit(solution)/shard_map/dot_general | solution.py:71
  539.9 1.4 pad_maximum_fusion.2
  541.2 0.0 copy-done.1
  (3 shorter events, 0.0 us)
Async XLA Ops:
  7.4 378.9 %copy-start = (s32[1,4]{1,0:T(1,128)S(1)}, s32[1,4]{1,0:T(1,128)}, u32[]{:S(2)}) copy-start(s32[1,4]{1,0:T(1,128)} %param.10) | copy-start | bytes 52
  7.4 369.1 %copy-start.3 = (s32[1,4,4]{2,1,0:T(4,128)S(1)}, s32[1,4,4]{2,1,0:T(4,128)}, u32[]{:S(2)}) copy-start(s32[1,4,4]{2,1,0:T(4,128)} %param.9) | copy-start | bytes 196
  7.4 368.5 %all-gather.5.cloned.1.call-start = ((), (), s32[]{:S(2)}) async-start(), calls=%async_computation.1 | async-start | bytes 21233664 | tf_op jit(solution)/shard_map/all_gather | solution.py:64
  10.6 370.8 %slice-start = ((s8[6291456]{0:T(1024)(128)(4,1)}), s8[2097152]{0:T(1024)(128)(4,1)S(1)}, s32[]{:S(2)}) async-start(s8[6291456]{0:T(1024)(128)(4,1)} %bitcast.62), calls=%async_computation.2 | async-start | bytes 4194304
  10.6 509.4 %all-gather.3.cloned.1.call-start = ((), (), s32[]{:S(2)}) async-start(), calls=%async_computation | async-start | bytes 4718592 | tf_op jit(solution)/shard_map/all_gather | solution.py:61
  375.9 144.1 %collective-permute-start.2 = (bf16[6144,1536]{1,0:T(8,128)(2,1)}, bf16[6144,1536]{1,0:T(8,128)(2,1)}, u32[]{:S(2)}, u32[]{:S(2)}) collective-permute-start(bf16[6144,1536]{1,0:T(8,128)(2,1)} %all-gather.5.cloned.1.call-done), channel_id=1, source_target_pairs={{0,1},{1,0},{2,3},{3,2},{4,5},{5,4},{6,7},{7,6},{8,9},{9,8},{10,11... | collective-permute-start | bytes 56623112 | tf_op jit(solution)/shard_map/ppermute | solution.py:16
  375.9 37.5 %collective-permute-start = (bf16[1,1024,3072]{2,1,0:T(8,128)(2,1)}, bf16[1,1024,3072]{2,1,0:T(8,128)(2,1)}, u32[]{:S(2)}, u32[]{:S(2)}) collective-permute-start(bf16[1,1024,3072]{2,1,0:T(8,128)(2,1)} %param.8), channel_id=1, source_target_pairs={{0,1},{1,0},{2,3},{3,2},{4,5},{5,4},{6,7},{7,6},{8,9},{9,8},{10,11... | collective-permute-start | bytes 18874376 | tf_op jit(solution)/shard_map/ppermute | solution.py:16
  376.4 46.0 %collective-permute-start.1 = (bf16[1,1024,3072]{2,1,0:T(8,128)(2,1)}, bf16[1,1024,3072]{2,1,0:T(8,128)(2,1)}, u32[]{:S(2)}, u32[]{:S(2)}) collective-permute-start(bf16[1,1024,3072]{2,1,0:T(8,128)(2,1)} %param.7), channel_id=1, source_target_pairs={{0,1},{1,0},{2,3},{3,2},{4,5},{5,4},{6,7},{7,6},{8,9},{9,8},{10,11... | collective-permute-start | bytes 18874376 | tf_op jit(solution)/shard_map/ppermute | solution.py:16
  376.5 4.9 slice-start.1
  381.4 4.5 copy-start.2
  529.9 11.3 %copy-start.1 = (s32[1,4]{1,0:T(1,128)S(1)}, s32[1,4]{1,0:T(1,128)}, u32[]{:S(2)}) copy-start(s32[1,4]{1,0:T(1,128)} %param.10) | copy-start | bytes 52
Sparse Core Ops, SparseCore 0:
  10.8 365.1 all-gather.4
Sparse Core Ops, SparseCore 1:
  475.2 44.7 all-gather.2
where the time goes:
time: 549 us
  waiting for transfers between devices  441 us (80%)
  local copies, waits for them, and re-layouts  44.6 us (8%)
  matrix products  29.5 us (5%)
  other arithmetic  17.7 us (3%)
  between operations  15 us (3%)
    all_gather x1, waiting for transfers between devices, local(): gathered = lax.all_gather(own_half, 'row', axis=0, tiled=True)  365 us
    all_gather x1, waiting for transfers between devices, local(): full_rows = lax.all_gather(heads_out, 'col', axis=1, tiled=True)  44.9 us
    ppermute x3, waiting for transfers between devices, swapped(): return lax.ppermute(value, axis, pairs)  31.2 us
    unnamed x18, local copies, waits for them, and re-layouts  23.2 us
  transfers between devices with their start and end apart: 5, of which 4 were waited for; matrix products, arithmetic and copies ran while one was open for 12% of the time, Pallas kernels for 0%

commit v1 on v0

v1 whole, which is shorter than its diff:
```python
import functools
import math

import jax
import jax.numpy as jnp
from jax import lax
from jax.experimental import pallas as pl
from jax.experimental.pallas import tpu as pltpu
from jax.sharding import PartitionSpec as P


HD = 128
BLK = 128
LIST = 4
PAIR = 2


def swapped(value, axis, mask):
    pairs = [(source, source ^ mask) for source in range(lax.axis_size(axis))]
    return lax.ppermute(value, axis, pairs)


def crossed(value, row_mask):
    count = lax.axis_size("row")
    pairs = [(2 * r + t, 2 * (r ^ row_mask) + 1 - t) for r in range(count) for t in range(2)]
    return lax.ppermute(value, ("row", "tm"), pairs)


def upper(row):
    return (row // PAIR) % 2


def handed(value):
    count = lax.axis_size("row")
    pairs = [
        (2 * r + 1 - upper(r), 2 * (r ^ PAIR) + 1 - upper(r ^ PAIR)) for r in range(count)
    ]
    return lax.ppermute(value, ("row", "tm"), pairs)


def attention_kernel(
    head_count, span, first, lists, counts, core, q_own, q_peer, k_own, v_own, k_peer, v_peer,
    out, k_buf, v_buf, k_sem, v_sem
):
    step = pl.program_id(0)
    block = first + step
    half = head_count * HD
    me = core[0]

    def copies(b, slot, j, mine):
        entry = lists[b * LIST + j]
        rows = pl.ds(pl.multiple_of(lax.rem(entry, span) * BLK, BLK), BLK)
        columns = pl.ds(pl.multiple_of(me * half, HD), half)
        place = pl.ds(j * BLK, BLK)
        k_from = k_own.at[rows, columns] if mine else k_peer.at[rows, :]
        v_from = v_own.at[rows, columns] if mine else v_peer.at[rows, :]
        return (
            pltpu.make_async_copy(k_from, k_buf.at[slot, place, :], k_sem.at[slot, j]),
            pltpu.make_async_copy(v_from, v_buf.at[slot, place, :], v_sem.at[slot, j]),
        )

    def fetch(b, slot):
        for j in range(LIST):
            mine = lax.div(lists[b * LIST + j], span) == me

            @pl.when(mine)
            def _():
                for copy in copies(b, slot, j, True):
                    copy.start()

            @pl.when(jnp.logical_not(mine))
            def _():
                for copy in copies(b, slot, j, False):
                    copy.start()

    slot = lax.rem(step, 2)

    @pl.when(step == 0)
    def _():
        fetch(block, slot)

    @pl.when(step + 1 < pl.num_programs(0))
    def _():
        fetch(block + 1, 1 - slot)

    for j in range(LIST):
        for copy in copies(block, slot, j, False):
            copy.wait()

    own = lax.div(first, pl.num_programs(0)) == me
    live = lax.broadcasted_iota(jnp.int32, (1, LIST * BLK), 1) < counts[block] * BLK
    scale = math.log2(math.e) / math.sqrt(HD)
    for head in range(head_count):
        part = slice(head * HD, (head + 1) * HD)
        query = jnp.where(own, q_own[:, part], q_peer[:, part])
        scores = lax.dot_general(
            query, k_buf[slot, :, part], (((1,), (1,)), ((), ())),
            preferred_element_type=jnp.float32,
        )
        power = jnp.minimum(math.log2(LIST * BLK) - scores * scale, 126.0)
        weights = 1.0 / (1.0 + jnp.exp2(power))
        weights = jnp.where(live, weights, 0.0).astype(jnp.bfloat16)
        mixed = jnp.dot(weights, v_buf[slot, :, part], preferred_element_type=jnp.float32)
        out[:, part] = mixed.astype(jnp.bfloat16)


def attend(span_index, lists, counts, core, queries, peer_queries, keys, values, peer_keys, peer_values):
    half = peer_queries.shape[1]
    blocks = queries.shape[0] // BLK
    span = keys.shape[0] // BLK

    def own_map(b, lists, counts, core):
        return (b, core[0])

    def peer_map(b, lists, counts, core):
        return (b, 0)

    anywhere = pl.BlockSpec(memory_space=pl.ANY)
    return pl.pallas_call(
        functools.partial(attention_kernel, half // HD, span, span_index * blocks),
        out_shape=jax.ShapeDtypeStruct((blocks * BLK, half), jnp.bfloat16),
        grid_spec=pltpu.PrefetchScalarGridSpec(
            num_scalar_prefetch=3,
            grid=(blocks,),
            in_specs=[
                pl.BlockSpec((BLK, half), own_map),
                pl.BlockSpec((BLK, half), peer_map),
                anywhere, anywhere, anywhere, anywhere,
            ],
            out_specs=pl.BlockSpec((BLK, half), lambda b, *_: (b, 0)),
            scratch_shapes=[
                pltpu.VMEM((2, LIST * BLK, half), jnp.bfloat16),
                pltpu.VMEM((2, LIST * BLK, half), jnp.bfloat16),
                pltpu.SemaphoreType.DMA((2, LIST)),
                pltpu.SemaphoreType.DMA((2, LIST)),
            ],
        ),
        cost_estimate=pl.CostEstimate(
            flops=4 * blocks * BLK * LIST * BLK * half,
            bytes_accessed=4 * blocks * LIST * BLK * half,
            transcendentals=blocks * BLK * LIST * BLK * half // HD,
        ),
        name="attention",
    )(lists, counts, core, queries, peer_queries, keys, values, peer_keys, peer_values)


def product_kernel(table, *refs):
    count = len(refs) - 13
    rows, weights, outs = refs[:4], refs[4 : 4 + count], refs[4 + count : 8 + count]
    a_buf, w_buf, total, a_sem, w_sem = refs[8 + count :]
    tile = outs[0].shape[0]
    depth = w_buf.shape[1]

    def copies(i):
        columns = pl.ds(pl.multiple_of(table[4 + i] * depth, HD), depth)
        taken = [
            pltpu.make_async_copy(
                row.at[:, columns], a_buf.at[i, pl.ds(s * tile, tile), :], a_sem.at[i, s]
            )
            for s, row in enumerate(rows)
        ]
        return [pltpu.make_async_copy(weights[i], w_buf.at[i], w_sem.at[i])] + taken

    for i in range(count):
        for copy in copies(i):
            copy.start()
    for i in range(count):
        for copy in copies(i):
            copy.wait()
        term = jnp.dot(a_buf[i], w_buf[i], preferred_element_type=jnp.float32)
        total[...] = term if i == 0 else total[...] + term
    for k, out in enumerate(outs):
        place = (table[k // 2] * 2 + lax.rem(table[2] + k + k // 2, 2)) * tile
        out[...] = total[pl.ds(pl.multiple_of(place, tile), tile), :].astype(jnp.bfloat16)


def products(table, rows, weights):
    count = len(weights)
    depth, width = weights[0].shape
    tile = rows[0].shape[0]
    anywhere = pl.BlockSpec(memory_space=pl.ANY)
    return pl.pallas_call(
        product_kernel,
        out_shape=[jax.ShapeDtypeStruct((tile, width), jnp.bfloat16)] * 4,
        grid_spec=pltpu.PrefetchScalarGridSpec(
            num_scalar_prefetch=1,
            grid=(1,),
            in_specs=[anywhere] * (4 + count),
            out_specs=[pl.BlockSpec((tile, width), lambda i, table: (0, 0))] * 4,
            scratch_shapes=[
                pltpu.VMEM((count, 4 * tile, depth), jnp.bfloat16),
                pltpu.VMEM((count, depth, width), jnp.bfloat16),
                pltpu.VMEM((4 * tile, width), jnp.float32),
                pltpu.SemaphoreType.DMA((count, 4)),
                pltpu.SemaphoreType.DMA((count,)),
            ],
        ),
        cost_estimate=pl.CostEstimate(
            flops=8 * tile * count * depth * width,
            bytes_accessed=2 * (4 * tile * (count * depth + width) + count * depth * width),
            transcendentals=0,
        ),
        name="products",
    )(table, *rows, *weights)


def plain_products(table, rows, weights):
    depth, width = weights[0].shape
    joined = jnp.zeros((depth * len(weights), width), weights[0].dtype)
    for i, weight in enumerate(weights):
        joined = lax.dynamic_update_slice_in_dim(joined, weight, table[4 + i] * depth, 0)
    stacked = jnp.stack(rows)
    outs = []
    for k in range(4):
        place = table[k // 2] * 2 + (table[2] + k + k // 2) % 2
        taken = lax.dynamic_index_in_dim(stacked, place, 0, keepdims=False)
        product = jnp.dot(taken, joined, preferred_element_type=jnp.float32)
        outs.append(product.astype(jnp.bfloat16))
    return outs


def chunks_of(half):
    sizes = []
    left = half
    while left > 0:
        size = 512 if left >= 1024 else min(256, left)
        sizes.append(size)
        left -= size
    return sizes


def local(queries, k_cache, v_cache, lists, counts, w_out):
    core = lax.axis_index("tm")
    row = lax.axis_index("row")
    col = lax.axis_index("col")
    row_count = lax.axis_size("row")
    col_count = lax.axis_size("col")
    width = queries.shape[1]
    half = width // 2
    depth = w_out.shape[0]
    assert row_count == 4 * col_count and half == 2 * depth
    mine = upper(row)

    masks = [1 << bit for bit in range(row_count.bit_length() - 1) if 1 << bit != PAIR][::-1]
    weights, sizes = [], chunks_of(half)
    for j, size in enumerate(sizes):
        start = core * half + sum(sizes[:j])
        blocks = [lax.dynamic_slice_in_dim(w_out, start, size, 1)]
        for mask in masks:
            moved = []
            for block in blocks:
                moved.append(swapped(block, "row", mask))
            blocks = blocks + moved
        weights.append(blocks)
    origins = [0]
    for mask in masks:
        origins = origins + [origin ^ mask for origin in origins]

    def sent(value):
        taken = lax.dynamic_slice_in_dim(value, (1 - core) * half, half, 1)
        return swapped(taken, "tm", 1)

    keys, values = k_cache[0], v_cache[0]
    peer_queries, peer_keys = sent(queries), sent(keys)
    peer_values = sent(values)
    holds_own = core == mine
    rows_here, rows_there = [], []
    for part in range(2):
        heads_out = attend(
            part, lists.reshape(-1), counts.reshape(-1), core.reshape(1), queries,
            peer_queries, keys, values, peer_keys, peer_values,
        )
        arrived = handed(heads_out)
        block = jnp.where(holds_own, heads_out, arrived)
        bit = 1
        while bit < col_count:
            other = swapped(block, "col", bit)
            low = (col // bit) % 2 == 0
            block = jnp.concatenate(
                [jnp.where(low, block, other), jnp.where(low, other, block)], 1
            )
            bit *= 2
        rows_here.append(block)
        rows_there.append(swapped(block, "tm", 1))

    places = [((row ^ o) // 4) * 2 + (row ^ o) % 2 for o in origins]
    pair_source = jnp.where(holds_own, 1, 0)
    table = jnp.stack([pair_source, 1 - pair_source, core, core] + places).astype(jnp.int32)
    multiply = products if depth % HD == 0 else plain_products

    near, far = [], []
    for blocks in weights:
        pair_same, pair_cross, own_cross, own_same = multiply(table, rows_here + rows_there, blocks)
        from_same = swapped(pair_same, "row", PAIR)
        from_cross = crossed(pair_cross, PAIR)
        from_core = swapped(own_cross, "tm", 1)
        near.append(own_same.astype(jnp.float32) + from_same.astype(jnp.float32))
        far.append(from_core.astype(jnp.float32) + from_cross.astype(jnp.float32))
    near = jnp.concatenate(near, 1)
    far = jnp.concatenate(far, 1)
    result = jnp.concatenate(
        [jnp.where(core == 0, near, far), jnp.where(core == 0, far, near)], 1
    )
    return result.astype(jnp.bfloat16)


def solution(mesh):
    placed = (
        P(("row", "tm"), "col"),
        P("row", "tm", "col"),
        P("row", "tm", "col"),
        P("row", None, None),
        P("row", None),
        P("row", "col"),
    )
    return jax.shard_map(
        local, mesh=mesh, in_specs=placed, out_specs=P(("row", "tm"), "col"), check_vma=False
    )
```

time: 549 us -> 225 us (0.41)
  waiting for transfers between devices: 441 us -> 111 us
  Pallas kernels: 0 us -> 51.8 us
  starting transfers between devices: 0.56 us -> 40.2 us
  matrix products: 29.5 us -> 0 us
  local copies, waits for them, and re-layouts: 44.6 us -> 17.2 us
  between operations: 15 us -> 0.48 us
  other arithmetic: 17.7 us -> 3.68 us
    all_gather x2 -> x0, waiting for transfers between devices: 410 us -> none  [the longest x1 365 us: local(): gathered = lax.all_gather(own_half, 'row', axis=0, tiled=True)]
    ppermute x3 -> x27, waiting for transfers between devices: 31.2 us -> 94.9 us  [swapped(): return lax.ppermute(value, axis, pairs)]
    pallas_call x0 -> x6, Pallas kernels: none -> 51.8 us  [the longest x4 31.5 us: products(): pl.pallas_call(product_kernel, out_shape=[jax.ShapeDtypeStruct((tile, wid...]
    ppermute x3 -> x27, starting transfers between devices: 0.51 us -> 35.5 us  [swapped(): return lax.ppermute(value, axis, pairs)]
    dot_general x3 -> x0, matrix products: 29.5 us -> none  [the longest x1 9.93 us: local(): jnp.dot(full_rows, high_half, preferred_element_type=jnp.float32)]
    unnamed x18 -> x48, local copies, waits for them, and re-layouts: 23.2 us -> 4.58 us
    gather x2 -> x0, local copies, waits for them, and re-layouts: 17.1 us -> none  [the longest x1 8.54 us: attend(): value_taken = value_blocks[block_index]]
    ppermute x0 -> x6, waiting for transfers between devices: none -> 16.5 us  [the longest x4 16.5 us: crossed(): return lax.ppermute(value, ('row', 'tm'), pairs)]
  transfers between devices with their start and end apart: 5 -> 33, of which waited for: 4 -> 13; matrix products, arithmetic and copies ran while one was open for 12% -> 5% of each run, Pallas kernels for 0% -> 19%
where the time goes in v1:
time: 225 us
  waiting for transfers between devices  111 us (49%)
  Pallas kernels  51.8 us (23%)
  starting transfers between devices  40.2 us (18%)
  local copies, waits for them, and re-layouts  17.2 us (8%)
  other arithmetic  3.68 us (2%)
    ppermute x27, waiting for transfers between devices, swapped(): return lax.ppermute(value, axis, pairs)  94.9 us
    ppermute x27, starting transfers between devices, swapped(): return lax.ppermute(value, axis, pairs)  35.5 us
    pallas_call x4, Pallas kernels, products(): pl.pallas_call(product_kernel, out_shape=[jax.ShapeDtypeStruct((tile, wid...  31.5 us
    pallas_call x2, Pallas kernels, attend(): pl.pallas_call(functools.partial(attention_kernel, half // HD, span, span...  20.2 us
    ppermute x4, waiting for transfers between devices, crossed(): return lax.ppermute(value, ('row', 'tm'), pairs)  16.5 us
    dynamic_slice x3, local copies, waits for them, and re-layouts, sent(): taken = lax.dynamic_slice_in_dim(value, (1 - core) * half, half, 1)  6.81 us
    dynamic_slice x2, local copies, waits for them, and re-layouts, local(): blocks = [lax.dynamic_slice_in_dim(w_out, start, size, 1)]  4.62 us
    unnamed x48, local copies, waits for them, and re-layouts  4.58 us
  transfers between devices with their start and end apart: 33, of which 13 were waited for; matrix products, arithmetic and copies ran while one was open for 5% of the time, Pallas kernels for 19%

profile of v1, /device:TPU:0, one launch (start us, length us, event | category | flops | bytes accessed | tf_op | source)
XLA Modules:
  0.0 224.7 jit_solution(9007403623515789302)
XLA Ops:
  0.0 3.9 %dynamic-slice_bitcast_fusion.1 = bf16[1024,1536]{1,0:T(8,128)(2,1)} fusion(bf16[1,1024,3072]{2,1,0:T(8,128)(2,1)} %param.7, s32[]{:T(128)S(6)} %select_n.125), kind=kLoop, calls=%fused_computation.1 | loop fusion | bytes 6291460 | tf_op jit(solution)/shard_map/dynamic_slice | solution.py:260
  3.9 0.5 collective-permute-start.1
  4.4 0.4 copy-done
  4.9 2.0 dynamic-slice_bitcast_fusion
  6.8 0.5 collective-permute-start.2
  7.3 0.9 constant_dynamic-slice_fusion.4
  8.3 0.6 reshape.12.lists
  8.9 6.8 %collective-permute-done.q_peer = bf16[256,1536]{1,0:T(8,128)(2,1)} collective-permute-done((bf16[256,1536]{1,0:T(8,128)(2,1)}, bf16[256,1536]{1,0:T(8,128)(2,1)}, u32[]{:S(2)}, u32[]{:S(2)}) %collective-permute-start) | collective-permute-done | bytes 786464 | tf_op jit(solution)/shard_map/ppermute | solution.py:20
  15.7 1.7 copy-done.3
  17.4 10.0 %attention.3 = bf16[256,1536]{1,0:T(8,128)(2,1)} custom-call(s32[16]{0:T(128)} %reshape.12.lists, s32[4]{0:T(128)} %bitcast.18, s32[1]{0:T(128)} %bitcast.2.core, bf16[256,3072]{1,0:T(8,128)(2,1)} %q_own.3, bf16[256,1536]{1,0:T(8,128)(2,1)} %collective-permute-done.q_peer, bf16[1024,3072]{1,0:T(8,128)(2,1)} %bitcast.14, bf16[1024,3072]{1,0:T(8,128)(2,1)} %bitcast.16, ...), custom_call_target="tpu_custom_call" | custom-call | flops 805306368 | bytes 6291456 | tf_op jit(solution)/shard_map/attention/pallas_call | solution.py:119
  27.4 0.7 collective-permute-start.5
  28.2 10.2 %attention.2 = bf16[256,1536]{1,0:T(8,128)(2,1)} custom-call(s32[16]{0:T(128)} %reshape.12.lists, s32[4]{0:T(128)} %bitcast.19, s32[1]{0:T(128)} %bitcast.2.core, bf16[256,3072]{1,0:T(8,128)(2,1)} %q_own.3, bf16[256,1536]{1,0:T(8,128)(2,1)} %collective-permute-done.q_peer, bf16[1024,3072]{1,0:T(8,128)(2,1)} %bitcast.15, bf16[1024,3072]{1,0:T(8,128)(2,1)} %bitcast.17, ...), custom_call_target="tpu_custom_call" | custom-call | flops 805306368 | bytes 6291456 | tf_op jit(solution)/shard_map/attention/pallas_call | solution.py:119
  38.4 0.9 collective-permute-start.3
  39.3 0.1 broadcast_select_fusion
  39.4 2.9 %collective-permute-start.6 = (bf16[256,1536]{1,0:T(8,128)(2,1)S(1)}, bf16[256,1536]{1,0:T(8,128)(2,1)S(1)}, u32[]{:S(2)}, u32[]{:S(2)}) collective-permute-start(bf16[256,1536]{1,0:T(8,128)(2,1)S(1)} %broadcast_select_fusion), channel_id=1, source_target_pairs={{0,2},{2,0},{1,3},{3,1},{4,6},{6,4},{5,7},{7,5},{8,10},{10,8},{9,1... | collective-permute-start | bytes 2359304 | tf_op jit(solution)/shard_map/ppermute | solution.py:20
  42.3 2.7 %constant_dynamic-slice_fusion.3 = (bf16[768,512]{1,0:T(8,128)(2,1)}, bf16[768,512]{1,0:T(8,128)(2,1)}) fusion(bf16[768,3072]{1,0:T(8,128)(2,1)} %param.11, s32[]{:T(128)S(6)} %select_n.132, s32[]{:T(128)S(6)} %select_n.133), kind=kLoop, calls=%fused_computation.26 | loop fusion | bytes 3145736 | tf_op jit(solution)/shard_map/dynamic_slice | solution.py:248
  45.0 2.6 %collective-permute-start.9 = (bf16[768,512]{1,0:T(8,128)(2,1)}, bf16[768,512]{1,0:T(8,128)(2,1)}, u32[]{:S(2)}, u32[]{:S(2)}) collective-permute-start(bf16[768,512]{1,0:T(8,128)(2,1)} %get-tuple-element.37.refs_4_), channel_id=1, source_target_pairs={{0,16},{4,20},{8,24},{12,28},{16,0},{20,4},{24,8},{28,12},{1,17},{... | collective-permute-start | bytes 2359304 | tf_op jit(solution)/shard_map/ppermute | solution.py:20
  47.6 1.9 constant_dynamic-slice_fusion.1
  49.5 0.3 collective-permute-start.17
  49.9 0.1 broadcast_select_fusion.1
  50.0 0.3 collective-permute-start.4
  50.3 6.4 %collective-permute-done.6 = bf16[256,1536]{1,0:T(8,128)(2,1)S(1)} collective-permute-done((bf16[256,1536]{1,0:T(8,128)(2,1)S(1)}, bf16[256,1536]{1,0:T(8,128)(2,1)S(1)}, u32[]{:S(2)}, u32[]{:S(2)}) %collective-permute-start.6) | collective-permute-done | bytes 786464 | tf_op jit(solution)/shard_map/ppermute | solution.py:20
  56.7 0.1 broadcast_select_fusion.3
  56.8 0.2 pad_maximum_fusion.1.refs_1_
  57.1 9.0 %collective-permute-start.8 = (bf16[256,3072]{1,0:T(8,128)(2,1)S(1)}, bf16[256,3072]{1,0:T(8,128)(2,1)}, u32[]{:S(2)}, u32[]{:S(2)}) collective-permute-start(bf16[256,3072]{1,0:T(8,128)(2,1)S(1)} %pad_maximum_fusion.1.refs_1_), channel_id=1, source_target_pairs={{0,1},{1,0},{2,3},{3,2},{4,5},{5,4},{6,7},{7,6},{8,9},{9,8},{10,11... | collective-permute-start | bytes 4718600 | tf_op jit(solution)/shard_map/ppermute | solution.py:20
  66.1 5.4 %collective-permute-done.4 = bf16[256,1536]{1,0:T(8,128)(2,1)S(1)} collective-permute-done((bf16[256,1536]{1,0:T(8,128)(2,1)S(1)}, bf16[256,1536]{1,0:T(8,128)(2,1)S(1)}, u32[]{:S(2)}, u32[]{:S(2)}) %collective-permute-start.4) | collective-permute-done | bytes 786464 | tf_op jit(solution)/shard_map/ppermute | solution.py:20
  71.5 0.1 broadcast_select_fusion.5
  71.6 0.2 pad_maximum_fusion.refs_0_
  71.8 6.4 %collective-permute-start.7 = (bf16[256,3072]{1,0:T(8,128)(2,1)S(1)}, bf16[256,3072]{1,0:T(8,128)(2,1)}, u32[]{:S(2)}, u32[]{:S(2)}) collective-permute-start(bf16[256,3072]{1,0:T(8,128)(2,1)S(1)} %pad_maximum_fusion.refs_0_), channel_id=1, source_target_pairs={{0,1},{1,0},{2,3},{3,2},{4,5},{5,4},{6,7},{7,6},{8,9},{9,8},{10,11... | collective-permute-start | bytes 4718600 | tf_op jit(solution)/shard_map/ppermute | solution.py:20
  78.2 2.3 %collective-permute-start.10 = (bf16[768,512]{1,0:T(8,128)(2,1)}, bf16[768,512]{1,0:T(8,128)(2,1)S(1)}, u32[]{:S(2)}, u32[]{:S(2)}) collective-permute-start(bf16[768,512]{1,0:T(8,128)(2,1)} %get-tuple-element.37.refs_4_), channel_id=1, source_target_pairs={{0,4},{4,0},{8,12},{12,8},{16,20},{20,16},{24,28},{28,24},{1,5},{5... | collective-permute-start | bytes 2359304 | tf_op jit(solution)/shard_map/ppermute | solution.py:20
  80.5 18.3 %collective-permute-done.17.refs_5_ = bf16[768,256]{1,0:T(8,128)(2,1)} collective-permute-done((bf16[768,256]{1,0:T(8,128)(2,1)}, bf16[768,256]{1,0:T(8,128)(2,1)}, u32[]{:S(2)}, u32[]{:S(2)}) %collective-permute-start.17) | collective-permute-done | bytes 393248 | tf_op jit(solution)/shard_map/ppermute | solution.py:20
  98.7 1.7 collective-permute-start.11
  100.4 0.3 collective-permute-start.14
  100.8 34.0 %collective-permute-done.13.refs_5_ = bf16[768,512]{1,0:T(8,128)(2,1)} collective-permute-done((bf16[768,512]{1,0:T(8,128)(2,1)}, bf16[768,512]{1,0:T(8,128)(2,1)}, u32[]{:S(2)}, u32[]{:S(2)}) %collective-permute-start.13) | collective-permute-done | bytes 786464 | tf_op jit(solution)/shard_map/ppermute | solution.py:20
  134.7 1.6 collective-permute-start.15
  136.4 0.9 copy-done.17
  137.3 0.6 stack.32.table
  137.9 0.4 collective-permute-start.18
  138.3 1.6 collective-permute-start.19
  139.9 8.0 %products.4 = (bf16[256,512]{1,0:T(8,128)(2,1)}, bf16[256,512]{1,0:T(8,128)(2,1)}, bf16[256,512]{1,0:T(8,128)(2,1)}, bf16[256,512]{1,0:T(8,128)(2,1)}) custom-call(s32[8]{0:T(128)} %stack.32.table, bf16[256,3072]{1,0:T(8,128)(2,1)} %copy-done.2, bf16[256,3072]{1,0:T(8,128)(2,1)} %copy-done.1, bf16[256,3072]{1,0:T(8,128)(2,1)} %collective-permute-done.7.refs_2_, ...), custom_call_target="tpu_custom_call" | custom-call | flops 3221225472 | bytes 10485760 | tf_op jit(solution)/shard_map/products/pallas_call | solution.py:182
  147.9 8.8 %collective-permute-done.21.refs_5_ = bf16[768,256]{1,0:T(8,128)(2,1)} collective-permute-done((bf16[768,256]{1,0:T(8,128)(2,1)S(1)}, bf16[768,256]{1,0:T(8,128)(2,1)}, u32[]{:S(2)}, u32[]{:S(2)}) %collective-permute-start.21) | collective-permute-done | bytes 393248 | tf_op jit(solution)/shard_map/ppermute | solution.py:20
  156.7 0.4 collective-permute-start.22
  157.2 1.6 collective-permute-start.23
  158.8 8.0 %products.5 = (bf16[256,512]{1,0:T(8,128)(2,1)}, bf16[256,512]{1,0:T(8,128)(2,1)}, bf16[256,512]{1,0:T(8,128)(2,1)}, bf16[256,512]{1,0:T(8,128)(2,1)}) custom-call(s32[8]{0:T(128)} %stack.32.table, bf16[256,3072]{1,0:T(8,128)(2,1)} %copy-done.2, bf16[256,3072]{1,0:T(8,128)(2,1)} %copy-done.1, bf16[256,3072]{1,0:T(8,128)(2,1)} %collective-permute-done.7.refs_2_, ...), custom_call_target="tpu_custom_call" | custom-call | flops 3221225472 | bytes 10485760 | tf_op jit(solution)/shard_map/products/pallas_call | solution.py:182
  166.8 2.1 collective-permute-start.16
  168.9 3.3 %collective-permute-done.19.refs_7_ = bf16[768,256]{1,0:T(8,128)(2,1)S(1)} collective-permute-done((bf16[768,256]{1,0:T(8,128)(2,1)}, bf16[768,256]{1,0:T(8,128)(2,1)S(1)}, u32[]{:S(2)}, u32[]{:S(2)}) %collective-permute-start.19) | collective-permute-done | bytes 393248 | tf_op jit(solution)/shard_map/ppermute | solution.py:20
  172.2 0.8 copy-done.11
  173.0 7.7 %products.6 = (bf16[256,256]{1,0:T(8,128)(2,1)}, bf16[256,256]{1,0:T(8,128)(2,1)}, bf16[256,256]{1,0:T(8,128)(2,1)}, bf16[256,256]{1,0:T(8,128)(2,1)}) custom-call(s32[8]{0:T(128)} %stack.32.table, bf16[256,3072]{1,0:T(8,128)(2,1)} %copy-done.2, bf16[256,3072]{1,0:T(8,128)(2,1)} %copy-done.1, bf16[256,3072]{1,0:T(8,128)(2,1)} %collective-permute-done.7.refs_2_, ...), custom_call_target="tpu_custom_call" | custom-call | flops 1610612736 | bytes 8388608 | tf_op jit(solution)/shard_map/products/pallas_call | solution.py:182
  180.9 7.4 %collective-permute-done.23.refs_7_ = bf16[768,256]{1,0:T(8,128)(2,1)S(1)} collective-permute-done((bf16[768,256]{1,0:T(8,128)(2,1)}, bf16[768,256]{1,0:T(8,128)(2,1)S(1)}, u32[]{:S(2)}, u32[]{:S(2)}) %collective-permute-start.23) | collective-permute-done | bytes 393248 | tf_op jit(solution)/shard_map/ppermute | solution.py:20
  188.2 0.8 copy-done.10
  189.0 7.8 %products.7 = (bf16[256,256]{1,0:T(8,128)(2,1)}, bf16[256,256]{1,0:T(8,128)(2,1)}, bf16[256,256]{1,0:T(8,128)(2,1)}, bf16[256,256]{1,0:T(8,128)(2,1)}) custom-call(s32[8]{0:T(128)} %stack.32.table, bf16[256,3072]{1,0:T(8,128)(2,1)} %copy-done.2, bf16[256,3072]{1,0:T(8,128)(2,1)} %copy-done.1, bf16[256,3072]{1,0:T(8,128)(2,1)} %collective-permute-done.7.refs_2_, ...), custom_call_target="tpu_custom_call" | custom-call | flops 1610612736 | bytes 8388608 | tf_op jit(solution)/shard_map/products/pallas_call | solution.py:182
  197.0 0.5 collective-permute-start.29
  197.5 4.5 %collective-permute-done.24 = bf16[256,256]{1,0:T(8,128)(2,1)S(1)} collective-permute-done((bf16[256,256]{1,0:T(8,128)(2,1)}, bf16[256,256]{1,0:T(8,128)(2,1)S(1)}, u32[]{:S(2)}, u32[]{:S(2)}) %collective-permute-start.24) | collective-permute-done | bytes 131104 | tf_op jit(solution)/shard_map/ppermute | solution.py:20
  202.0 0.9 convert_add_fusion.6
  203.0 0.2 collective-permute-start.31
  203.2 3.3 %collective-permute-done.30 = bf16[256,256]{1,0:T(8,128)(2,1)S(1)} collective-permute-done((bf16[256,256]{1,0:T(8,128)(2,1)S(1)}, bf16[256,256]{1,0:T(8,128)(2,1)S(1)}, u32[]{:S(2)}, u32[]{:S(2)}) %collective-permute-start.30) | collective-permute-done | bytes 131104 | tf_op jit(solution)/shard_map/ppermute | solution.py:26
  206.4 0.8 collective-permute-start.32
  207.3 1.0 collective-permute-start.26
  208.3 4.1 %collective-permute-done.32 = bf16[256,256]{1,0:T(8,128)(2,1)S(1)} collective-permute-done((bf16[256,256]{1,0:T(8,128)(2,1)}, bf16[256,256]{1,0:T(8,128)(2,1)S(1)}, u32[]{:S(2)}, u32[]{:S(2)}) %collective-permute-start.32) | collective-permute-done | bytes 131104 | tf_op jit(solution)/shard_map/ppermute | solution.py:26
  212.5 1.2 collective-permute-start.28
  213.9 4.2 %collective-permute-done.26 = bf16[256,512]{1,0:T(8,128)(2,1)S(1)} collective-permute-done((bf16[256,512]{1,0:T(8,128)(2,1)S(1)}, bf16[256,512]{1,0:T(8,128)(2,1)S(1)}, u32[]{:S(2)}, u32[]{:S(2)}) %collective-permute-start.26) | collective-permute-done | bytes 262176 | tf_op jit(solution)/shard_map/ppermute | solution.py:26
  218.1 4.9 %collective-permute-done.28 = bf16[256,512]{1,0:T(8,128)(2,1)S(1)} collective-permute-done((bf16[256,512]{1,0:T(8,128)(2,1)S(1)}, bf16[256,512]{1,0:T(8,128)(2,1)S(1)}, u32[]{:S(2)}, u32[]{:S(2)}) %collective-permute-start.28) | collective-permute-done | bytes 262176 | tf_op jit(solution)/shard_map/ppermute | solution.py:26
  223.1 0.3 select_convert_fusion.1
  223.4 1.3 pad_maximum_fusion.4
  (79 shorter events, 0.8 us)
Async XLA Ops:
  0.0 4.9 %copy-start = (bf16[1,1024,3072]{2,1,0:T(8,128)(2,1)S(1)}, bf16[1,1024,3072]{2,1,0:T(8,128)(2,1)}, u32[]{:S(2)}) copy-start(bf16[1,1024,3072]{2,1,0:T(8,128)(2,1)} %param.8) | copy-start | bytes 18874372
  3.9 3.4 %copy-start.4 = (bf16[256,3072]{1,0:T(8,128)(2,1)S(1)}, bf16[256,3072]{1,0:T(8,128)(2,1)}, u32[]{:S(2)}) copy-start(bf16[256,3072]{1,0:T(8,128)(2,1)} %q_own.3) | copy-start | bytes 4718596
  3.9 11.7 %collective-permute-start.1 = (bf16[1024,1536]{1,0:T(8,128)(2,1)}, bf16[1024,1536]{1,0:T(8,128)(2,1)S(1)}, u32[]{:S(2)}, u32[]{:S(2)}) collective-permute-start(bf16[1024,1536]{1,0:T(8,128)(2,1)} %dynamic-slice_bitcast_fusion.1), channel_id=1, source_target_pairs={{0,1},{1,0},{2,3},{3,2},{4,5},{5,4},{6,7},{7,6},{8,9},{9,8},{10,11... | collective-permute-start | bytes 9437192 | tf_op jit(solution)/shard_map/ppermute | solution.py:20
  6.8 1.4 copy-start.15
  6.8 8.9 %collective-permute-start.2 = (bf16[1024,1536]{1,0:T(8,128)(2,1)}, bf16[1024,1536]{1,0:T(8,128)(2,1)}, u32[]{:S(2)}, u32[]{:S(2)}) collective-permute-start(bf16[1024,1536]{1,0:T(8,128)(2,1)} %dynamic-slice_bitcast_fusion), channel_id=1, source_target_pairs={{0,1},{1,0},{2,3},{3,2},{4,5},{5,4},{6,7},{7,6},{8,9},{9,8},{10,11... | collective-permute-start | bytes 9437192 | tf_op jit(solution)/shard_map/ppermute | solution.py:20
  8.2 7.4 %collective-permute-start = (bf16[256,1536]{1,0:T(8,128)(2,1)}, bf16[256,1536]{1,0:T(8,128)(2,1)}, u32[]{:S(2)}, u32[]{:S(2)}) collective-permute-start(bf16[256,1536]{1,0:T(8,128)(2,1)} %constant_dynamic-slice_fusion.4), channel_id=1, source_target_pairs={{0,1},{1,0},{2,3},{3,2},{4,5},{5,4},{6,7},{7,6},{8,9},{9,8},{10,11... | collective-permute-start | bytes 2359304 | tf_op jit(solution)/shard_map/ppermute | solution.py:20
  15.7 1.7 copy-start.3
  27.4 11.9 %collective-permute-start.5 = (bf16[256,1536]{1,0:T(8,128)(2,1)}, bf16[256,1536]{1,0:T(8,128)(2,1)S(1)}, u32[]{:S(2)}, u32[]{:S(2)}) collective-permute-start(bf16[256,1536]{1,0:T(8,128)(2,1)} %attention.3), channel_id=1, source_target_pairs={{1,8},{5,12},{8,1},{12,5},{17,24},{21,28},{24,17},{28,21},{3,10},{... | collective-permute-start | bytes 2359304 | tf_op jit(solution)/shard_map/ppermute | solution.py:38
  28.2 11.1 %copy-start.6 = (bf16[256,1536]{1,0:T(8,128)(2,1)S(1)}, bf16[256,1536]{1,0:T(8,128)(2,1)}, u32[]{:S(2)}) copy-start(bf16[256,1536]{1,0:T(8,128)(2,1)} %attention.3) | copy-start | bytes 2359300
  38.4 11.5 %collective-permute-start.3 = (bf16[256,1536]{1,0:T(8,128)(2,1)}, bf16[256,1536]{1,0:T(8,128)(2,1)S(1)}, u32[]{:S(2)}, u32[]{:S(2)}) collective-permute-start(bf16[256,1536]{1,0:T(8,128)(2,1)} %attention.2), channel_id=1, source_target_pairs={{1,8},{5,12},{8,1},{12,5},{17,24},{21,28},{24,17},{28,21},{3,10},{... | collective-permute-start | bytes 2359304 | tf_op jit(solution)/shard_map/ppermute | solution.py:38
  39.4 17.3 %collective-permute-start.6 = (bf16[256,1536]{1,0:T(8,128)(2,1)S(1)}, bf16[256,1536]{1,0:T(8,128)(2,1)S(1)}, u32[]{:S(2)}, u32[]{:S(2)}) collective-permute-start(bf16[256,1536]{1,0:T(8,128)(2,1)S(1)} %broadcast_select_fusion), channel_id=1, source_target_pairs={{0,2},{2,0},{1,3},{3,1},{4,6},{6,4},{5,7},{7,5},{8,10},{10,8},{9,1... | collective-permute-start | bytes 2359304 | tf_op jit(solution)/shard_map/ppermute | solution.py:20
  45.0 4.9 %copy-start.5 = (bf16[256,1536]{1,0:T(8,128)(2,1)S(1)}, bf16[256,1536]{1,0:T(8,128)(2,1)}, u32[]{:S(2)}) copy-start(bf16[256,1536]{1,0:T(8,128)(2,1)} %attention.2) | copy-start | bytes 2359300
  45.0 53.7 %collective-permute-start.9 = (bf16[768,512]{1,0:T(8,128)(2,1)}, bf16[768,512]{1,0:T(8,128)(2,1)}, u32[]{:S(2)}, u32[]{:S(2)}) collective-permute-start(bf16[768,512]{1,0:T(8,128)(2,1)} %get-tuple-element.37.refs_4_), channel_id=1, source_target_pairs={{0,16},{4,20},{8,24},{12,28},{16,0},{20,4},{24,8},{28,12},{1,17},{... | collective-permute-start | bytes 2359304 | tf_op jit(solution)/shard_map/ppermute | solution.py:20
  49.5 107.2 %copy-start.7 = (bf16[768,256]{1,0:T(8,128)(2,1)}, bf16[768,256]{1,0:T(8,128)(2,1)S(1)}, u32[]{:S(2)}) copy-start(bf16[768,256]{1,0:T(8,128)(2,1)S(1)} %get-tuple-element.40.refs_4_) | copy-start | bytes 1179652
  49.5 49.2 %collective-permute-start.17 = (bf16[768,256]{1,0:T(8,128)(2,1)}, bf16[768,256]{1,0:T(8,128)(2,1)}, u32[]{:S(2)}, u32[]{:S(2)}) collective-permute-start(bf16[768,256]{1,0:T(8,128)(2,1)} %get-tuple-element.39.refs_4_), channel_id=1, source_target_pairs={{0,16},{4,20},{8,24},{12,28},{16,0},{20,4},{24,8},{28,12},{1,17},{... | collective-permute-start | bytes 1179656 | tf_op jit(solution)/shard_map/ppermute | solution.py:20
  50.0 21.5 %collective-permute-start.4 = (bf16[256,1536]{1,0:T(8,128)(2,1)S(1)}, bf16[256,1536]{1,0:T(8,128)(2,1)S(1)}, u32[]{:S(2)}, u32[]{:S(2)}) collective-permute-start(bf16[256,1536]{1,0:T(8,128)(2,1)S(1)} %broadcast_select_fusion.1), channel_id=1, source_target_pairs={{0,2},{2,0},{1,3},{3,1},{4,6},{6,4},{5,7},{7,5},{8,10},{10,8},{9,1... | collective-permute-start | bytes 2359304 | tf_op jit(solution)/shard_map/ppermute | solution.py:20
  57.0 14.6 %copy-start.1 = (bf16[256,3072]{1,0:T(8,128)(2,1)}, bf16[256,3072]{1,0:T(8,128)(2,1)S(1)}, u32[]{:S(2)}) copy-start(bf16[256,3072]{1,0:T(8,128)(2,1)S(1)} %pad_maximum_fusion.1.refs_1_) | copy-start | bytes 4718596
  57.1 80.8 %collective-permute-start.8 = (bf16[256,3072]{1,0:T(8,128)(2,1)S(1)}, bf16[256,3072]{1,0:T(8,128)(2,1)}, u32[]{:S(2)}, u32[]{:S(2)}) collective-permute-start(bf16[256,3072]{1,0:T(8,128)(2,1)S(1)} %pad_maximum_fusion.1.refs_1_), channel_id=1, source_target_pairs={{0,1},{1,0},{2,3},{3,2},{4,5},{5,4},{6,7},{7,6},{8,9},{9,8},{10,11... | collective-permute-start | bytes 4718600 | tf_op jit(solution)/shard_map/ppermute | solution.py:20
  71.8 68.1 %copy-start.2 = (bf16[256,3072]{1,0:T(8,128)(2,1)}, bf16[256,3072]{1,0:T(8,128)(2,1)S(1)}, u32[]{:S(2)}) copy-start(bf16[256,3072]{1,0:T(8,128)(2,1)S(1)} %pad_maximum_fusion.refs_0_) | copy-start | bytes 4718596
  71.8 66.4 %collective-permute-start.7 = (bf16[256,3072]{1,0:T(8,128)(2,1)S(1)}, bf16[256,3072]{1,0:T(8,128)(2,1)}, u32[]{:S(2)}, u32[]{:S(2)}) collective-permute-start(bf16[256,3072]{1,0:T(8,128)(2,1)S(1)} %pad_maximum_fusion.refs_0_), channel_id=1, source_target_pairs={{0,1},{1,0},{2,3},{3,2},{4,5},{5,4},{6,7},{7,6},{8,9},{9,8},{10,11... | collective-permute-start | bytes 4718600 | tf_op jit(solution)/shard_map/ppermute | solution.py:20
  78.2 22.2 %collective-permute-start.10 = (bf16[768,512]{1,0:T(8,128)(2,1)}, bf16[768,512]{1,0:T(8,128)(2,1)S(1)}, u32[]{:S(2)}, u32[]{:S(2)}) collective-permute-start(bf16[768,512]{1,0:T(8,128)(2,1)} %get-tuple-element.37.refs_4_), channel_id=1, source_target_pairs={{0,4},{4,0},{8,12},{12,8},{16,20},{20,16},{24,28},{28,24},{1,5},{5... | collective-permute-start | bytes 2359304 | tf_op jit(solution)/shard_map/ppermute | solution.py:20
  98.7 36.0 %collective-permute-start.13 = (bf16[768,512]{1,0:T(8,128)(2,1)}, bf16[768,512]{1,0:T(8,128)(2,1)}, u32[]{:S(2)}, u32[]{:S(2)}) collective-permute-start(bf16[768,512]{1,0:T(8,128)(2,1)} %get-tuple-element.38.refs_4_), channel_id=1, source_target_pairs={{0,16},{4,20},{8,24},{12,28},{16,0},{20,4},{24,8},{28,12},{1,17},{... | collective-permute-start | bytes 2359304 | tf_op jit(solution)/shard_map/ppermute | solution.py:20
  98.7 37.7 %collective-permute-start.11 = (bf16[768,512]{1,0:T(8,128)(2,1)}, bf16[768,512]{1,0:T(8,128)(2,1)S(1)}, u32[]{:S(2)}, u32[]{:S(2)}) collective-permute-start(bf16[768,512]{1,0:T(8,128)(2,1)} %collective-permute-done.9.refs_5_), channel_id=1, source_target_pairs={{0,4},{4,0},{8,12},{12,8},{16,20},{20,16},{24,28},{28,24},{1,5},{5... | collective-permute-start | bytes 2359304 | tf_op jit(solution)/shard_map/ppermute | solution.py:20
  100.4 36.0 %copy-start.16 = (bf16[768,512]{1,0:T(8,128)(2,1)}, bf16[768,512]{1,0:T(8,128)(2,1)S(1)}, u32[]{:S(2)}) copy-start(bf16[768,512]{1,0:T(8,128)(2,1)S(1)} %collective-permute-done.10.refs_6_) | copy-start | bytes 2359300
  100.4 56.7 %collective-permute-start.14 = (bf16[768,512]{1,0:T(8,128)(2,1)}, bf16[768,512]{1,0:T(8,128)(2,1)}, u32[]{:S(2)}, u32[]{:S(2)}) collective-permute-start(bf16[768,512]{1,0:T(8,128)(2,1)} %get-tuple-element.38.refs_4_), channel_id=1, source_target_pairs={{0,4},{4,0},{8,12},{12,8},{16,20},{20,16},{24,28},{28,24},{1,5},{5... | collective-permute-start | bytes 2359304 | tf_op jit(solution)/shard_map/ppermute | solution.py:20
  134.7 24.0 %collective-permute-start.15 = (bf16[768,512]{1,0:T(8,128)(2,1)}, bf16[768,512]{1,0:T(8,128)(2,1)}, u32[]{:S(2)}, u32[]{:S(2)}) collective-permute-start(bf16[768,512]{1,0:T(8,128)(2,1)} %collective-permute-done.13.refs_5_), channel_id=1, source_target_pairs={{0,4},{4,0},{8,12},{12,8},{16,20},{20,16},{24,28},{28,24},{1,5},{5... | collective-permute-start | bytes 2359304 | tf_op jit(solution)/shard_map/ppermute | solution.py:20
  136.4 0.9 copy-start.17
  137.3 19.5 %collective-permute-start.21 = (bf16[768,256]{1,0:T(8,128)(2,1)S(1)}, bf16[768,256]{1,0:T(8,128)(2,1)}, u32[]{:S(2)}, u32[]{:S(2)}) collective-permute-start(bf16[768,256]{1,0:T(8,128)(2,1)S(1)} %get-tuple-element.40.refs_4_), channel_id=1, source_target_pairs={{0,16},{4,20},{8,24},{12,28},{16,0},{20,4},{24,8},{28,12},{1,17},{... | collective-permute-start | bytes 1179656 | tf_op jit(solution)/shard_map/ppermute | solution.py:20
  137.9 28.9 %collective-permute-start.18 = (bf16[768,256]{1,0:T(8,128)(2,1)}, bf16[768,256]{1,0:T(8,128)(2,1)S(1)}, u32[]{:S(2)}, u32[]{:S(2)}) collective-permute-start(bf16[768,256]{1,0:T(8,128)(2,1)} %get-tuple-element.39.refs_4_), channel_id=1, source_target_pairs={{0,4},{4,0},{8,12},{12,8},{16,20},{20,16},{24,28},{28,24},{1,5},{5... | collective-permute-start | bytes 1179656 | tf_op jit(solution)/shard_map/ppermute | solution.py:20
  138.3 34.0 %collective-permute-start.19 = (bf16[768,256]{1,0:T(8,128)(2,1)}, bf16[768,256]{1,0:T(8,128)(2,1)S(1)}, u32[]{:S(2)}, u32[]{:S(2)}) collective-permute-start(bf16[768,256]{1,0:T(8,128)(2,1)} %collective-permute-done.17.refs_5_), channel_id=1, source_target_pairs={{0,4},{4,0},{8,12},{12,8},{16,20},{20,16},{24,28},{28,24},{1,5},{5... | collective-permute-start | bytes 1179656 | tf_op jit(solution)/shard_map/ppermute | solution.py:20
  156.7 24.1 %collective-permute-start.22 = (bf16[768,256]{1,0:T(8,128)(2,1)S(1)}, bf16[768,256]{1,0:T(8,128)(2,1)S(1)}, u32[]{:S(2)}, u32[]{:S(2)}) collective-permute-start(bf16[768,256]{1,0:T(8,128)(2,1)S(1)} %get-tuple-element.40.refs_4_), channel_id=1, source_target_pairs={{0,4},{4,0},{8,12},{12,8},{16,20},{20,16},{24,28},{28,24},{1,5},{5... | collective-permute-start | bytes 1179656 | tf_op jit(solution)/shard_map/ppermute | solution.py:20
  157.2 31.1 %collective-permute-start.23 = (bf16[768,256]{1,0:T(8,128)(2,1)}, bf16[768,256]{1,0:T(8,128)(2,1)S(1)}, u32[]{:S(2)}, u32[]{:S(2)}) collective-permute-start(bf16[768,256]{1,0:T(8,128)(2,1)} %collective-permute-done.21.refs_5_), channel_id=1, source_target_pairs={{0,4},{4,0},{8,12},{12,8},{16,20},{20,16},{24,28},{28,24},{1,5},{5... | collective-permute-start | bytes 1179656 | tf_op jit(solution)/shard_map/ppermute | solution.py:20
  158.8 53.7 %collective-permute-start.12 = (bf16[256,512]{1,0:T(8,128)(2,1)}, bf16[256,512]{1,0:T(8,128)(2,1)S(1)}, u32[]{:S(2)}, u32[]{:S(2)}) collective-permute-start(bf16[256,512]{1,0:T(8,128)(2,1)} %get-tuple-element.22), channel_id=1, source_target_pairs={{0,8},{4,12},{8,0},{12,4},{16,24},{20,28},{24,16},{28,20},{1,9},{5... | collective-permute-start | bytes 786440 | tf_op jit(solution)/shard_map/ppermute | solution.py:20
  166.8 5.4 %copy-start.9 = (bf16[768,256]{1,0:T(8,128)(2,1)}, bf16[768,256]{1,0:T(8,128)(2,1)S(1)}, u32[]{:S(2)}) copy-start(bf16[768,256]{1,0:T(8,128)(2,1)S(1)} %collective-permute-done.18.refs_6_) | copy-start | bytes 1179652
  166.8 46.9 %collective-permute-start.16 = (bf16[256,512]{1,0:T(8,128)(2,1)}, bf16[256,512]{1,0:T(8,128)(2,1)S(1)}, u32[]{:S(2)}, u32[]{:S(2)}) collective-permute-start(bf16[256,512]{1,0:T(8,128)(2,1)} %get-tuple-element.24), channel_id=1, source_target_pairs={{0,8},{4,12},{8,0},{12,4},{16,24},{20,28},{24,16},{28,20},{1,9},{5... | collective-permute-start | bytes 786440 | tf_op jit(solution)/shard_map/ppermute | solution.py:20
  172.2 0.8 copy-start.11
  180.7 16.2 %copy-start.19 = (bf16[256,512]{1,0:T(8,128)(2,1)S(1)}, bf16[256,512]{1,0:T(8,128)(2,1)}, u32[]{:S(2)}) copy-start(bf16[256,512]{1,0:T(8,128)(2,1)} %get-tuple-element.29) | copy-start | bytes 786436
  180.7 16.3 %copy-start.23 = (bf16[256,256]{1,0:T(8,128)(2,1)S(1)}, bf16[256,256]{1,0:T(8,128)(2,1)}, u32[]{:S(2)}) copy-start(bf16[256,256]{1,0:T(8,128)(2,1)} %get-tuple-element.33) | copy-start | bytes 393220
  180.7 16.7 %copy-start.14 = (bf16[256,256]{1,0:T(8,128)(2,1)S(1)}, bf16[256,256]{1,0:T(8,128)(2,1)}, u32[]{:S(2)}) copy-start(bf16[256,256]{1,0:T(8,128)(2,1)} %get-tuple-element.25) | copy-start | bytes 393220
  180.7 21.3 %copy-start.22 = (bf16[256,256]{1,0:T(8,128)(2,1)S(1)}, bf16[256,256]{1,0:T(8,128)(2,1)}, u32[]{:S(2)}) copy-start(bf16[256,256]{1,0:T(8,128)(2,1)} %get-tuple-element.34) | copy-start | bytes 393220
  180.7 26.6 %copy-start.18 = (bf16[256,512]{1,0:T(8,128)(2,1)S(1)}, bf16[256,512]{1,0:T(8,128)(2,1)}, u32[]{:S(2)}) copy-start(bf16[256,512]{1,0:T(8,128)(2,1)} %get-tuple-element.30) | copy-start | bytes 786436
  180.7 31.7 %copy-start.21 = (bf16[256,512]{1,0:T(8,128)(2,1)S(1)}, bf16[256,512]{1,0:T(8,128)(2,1)}, u32[]{:S(2)}) copy-start(bf16[256,512]{1,0:T(8,128)(2,1)} %get-tuple-element.31) | copy-start | bytes 786436
  180.8 16.2 %collective-permute-start.20 = (bf16[256,256]{1,0:T(8,128)(2,1)}, bf16[256,256]{1,0:T(8,128)(2,1)S(1)}, u32[]{:S(2)}, u32[]{:S(2)}) collective-permute-start(bf16[256,256]{1,0:T(8,128)(2,1)} %get-tuple-element.26), channel_id=1, source_target_pairs={{0,8},{4,12},{8,0},{12,4},{16,24},{20,28},{24,16},{28,20},{1,9},{5... | collective-permute-start | bytes 393224 | tf_op jit(solution)/shard_map/ppermute | solution.py:20
  180.8 7.4 %copy-start.8 = (bf16[768,256]{1,0:T(8,128)(2,1)}, bf16[768,256]{1,0:T(8,128)(2,1)S(1)}, u32[]{:S(2)}) copy-start(bf16[768,256]{1,0:T(8,128)(2,1)S(1)} %collective-permute-done.22.refs_6_) | copy-start | bytes 1179652
  188.2 0.8 copy-start.10
  196.8 15.7 %copy-start.20 = (bf16[256,512]{1,0:T(8,128)(2,1)S(1)}, bf16[256,512]{1,0:T(8,128)(2,1)}, u32[]{:S(2)}) copy-start(bf16[256,512]{1,0:T(8,128)(2,1)} %get-tuple-element.32) | copy-start | bytes 786436
  196.8 16.9 %copy-start.12 = (bf16[256,512]{1,0:T(8,128)(2,1)S(1)}, bf16[256,512]{1,0:T(8,128)(2,1)}, u32[]{:S(2)}) copy-start(bf16[256,512]{1,0:T(8,128)(2,1)} %get-tuple-element.21) | copy-start | bytes 786436
  196.8 17.0 %copy-start.13 = (bf16[256,512]{1,0:T(8,128)(2,1)S(1)}, bf16[256,512]{1,0:T(8,128)(2,1)}, u32[]{:S(2)}) copy-start(bf16[256,512]{1,0:T(8,128)(2,1)} %get-tuple-element.23) | copy-start | bytes 786436
  196.8 5.2 %collective-permute-start.24 = (bf16[256,256]{1,0:T(8,128)(2,1)}, bf16[256,256]{1,0:T(8,128)(2,1)S(1)}, u32[]{:S(2)}, u32[]{:S(2)}) collective-permute-start(bf16[256,256]{1,0:T(8,128)(2,1)} %get-tuple-element.28), channel_id=1, source_target_pairs={{0,8},{4,12},{8,0},{12,4},{16,24},{20,28},{24,16},{28,20},{1,9},{5... | collective-permute-start | bytes 393224 | tf_op jit(solution)/shard_map/ppermute | solution.py:20
  196.9 17.0 %collective-permute-start.25 = (bf16[256,512]{1,0:T(8,128)(2,1)S(1)}, bf16[256,512]{1,0:T(8,128)(2,1)S(1)}, u32[]{:S(2)}, u32[]{:S(2)}) collective-permute-start(bf16[256,512]{1,0:T(8,128)(2,1)S(1)} %copy-done.19), channel_id=1, source_target_pairs={{0,1},{1,0},{2,3},{3,2},{4,5},{5,4},{6,7},{7,6},{8,9},{9,8},{10,11... | collective-permute-start | bytes 786440 | tf_op jit(solution)/shard_map/ppermute | solution.py:20
  197.0 6.0 %collective-permute-start.29 = (bf16[256,256]{1,0:T(8,128)(2,1)S(1)}, bf16[256,256]{1,0:T(8,128)(2,1)S(1)}, u32[]{:S(2)}, u32[]{:S(2)}) collective-permute-start(bf16[256,256]{1,0:T(8,128)(2,1)S(1)} %copy-done.23), channel_id=1, source_target_pairs={{0,1},{1,0},{2,3},{3,2},{4,5},{5,4},{6,7},{7,6},{8,9},{9,8},{10,11... | collective-permute-start | bytes 393224 | tf_op jit(solution)/shard_map/ppermute | solution.py:20
  202.0 4.4 %collective-permute-start.30 = (bf16[256,256]{1,0:T(8,128)(2,1)S(1)}, bf16[256,256]{1,0:T(8,128)(2,1)S(1)}, u32[]{:S(2)}, u32[]{:S(2)}) collective-permute-start(bf16[256,256]{1,0:T(8,128)(2,1)S(1)} %copy-done.22), channel_id=1, source_target_pairs={{0,9},{1,8},{4,13},{5,12},{8,1},{9,0},{12,5},{13,4},{16,25},{17,24... | collective-permute-start | bytes 393224 | tf_op jit(solution)/shard_map/ppermute | solution.py:26
  203.0 4.3 %collective-permute-start.31 = (bf16[256,256]{1,0:T(8,128)(2,1)}, bf16[256,256]{1,0:T(8,128)(2,1)S(1)}, u32[]{:S(2)}, u32[]{:S(2)}) collective-permute-start(bf16[256,256]{1,0:T(8,128)(2,1)} %get-tuple-element.35), channel_id=1, source_target_pairs={{0,1},{1,0},{2,3},{3,2},{4,5},{5,4},{6,7},{7,6},{8,9},{9,8},{10,11... | collective-permute-start | bytes 393224 | tf_op jit(solution)/shard_map/ppermute | solution.py:20
  206.4 6.0 %collective-permute-start.32 = (bf16[256,256]{1,0:T(8,128)(2,1)}, bf16[256,256]{1,0:T(8,128)(2,1)S(1)}, u32[]{:S(2)}, u32[]{:S(2)}) collective-permute-start(bf16[256,256]{1,0:T(8,128)(2,1)} %get-tuple-element.36), channel_id=1, source_target_pairs={{0,9},{1,8},{4,13},{5,12},{8,1},{9,0},{12,5},{13,4},{16,25},{17,24... | collective-permute-start | bytes 393224 | tf_op jit(solution)/shard_map/ppermute | solution.py:26
  207.3 10.7 %collective-permute-start.26 = (bf16[256,512]{1,0:T(8,128)(2,1)S(1)}, bf16[256,512]{1,0:T(8,128)(2,1)S(1)}, u32[]{:S(2)}, u32[]{:S(2)}) collective-permute-start(bf16[256,512]{1,0:T(8,128)(2,1)S(1)} %copy-done.18), channel_id=1, source_target_pairs={{0,9},{1,8},{4,13},{5,12},{8,1},{9,0},{12,5},{13,4},{16,25},{17,24... | collective-permute-start | bytes 786440 | tf_op jit(solution)/shard_map/ppermute | solution.py:26
  212.4 5.7 %collective-permute-start.27 = (bf16[256,512]{1,0:T(8,128)(2,1)S(1)}, bf16[256,512]{1,0:T(8,128)(2,1)S(1)}, u32[]{:S(2)}, u32[]{:S(2)}) collective-permute-start(bf16[256,512]{1,0:T(8,128)(2,1)S(1)} %copy-done.21), channel_id=1, source_target_pairs={{0,1},{1,0},{2,3},{3,2},{4,5},{5,4},{6,7},{7,6},{8,9},{9,8},{10,11... | collective-permute-start | bytes 786440 | tf_op jit(solution)/shard_map/ppermute | solution.py:20
  212.5 10.6 %collective-permute-start.28 = (bf16[256,512]{1,0:T(8,128)(2,1)S(1)}, bf16[256,512]{1,0:T(8,128)(2,1)S(1)}, u32[]{:S(2)}, u32[]{:S(2)}) collective-permute-start(bf16[256,512]{1,0:T(8,128)(2,1)S(1)} %copy-done.20), channel_id=1, source_target_pairs={{0,9},{1,8},{4,13},{5,12},{8,1},{9,0},{12,5},{13,4},{16,25},{17,24... | collective-permute-start | bytes 786440 | tf_op jit(solution)/shard_map/ppermute | solution.py:26
